TPU v7x, 32 devices: a whole 2x2x4 slice. The times are simulated.
32 devices in a mesh: dp: 8 (over y, x, core), head: 4 (over z).
Axes of the slice: x: 2, y: 2, z: 4, core: 2. Of those that a mesh axis runs over, the one named last changes fastest.
Arguments:
- tokens: bfloat16 [6400, 384], P(('dp', 'head')), may hold values from -6 to 6
- grad_out: bfloat16 [1600, 768], P(('dp', 'head')), may hold values from -6 to 6
- video_ids: int32 [16], replicated, may hold values from 0 to 3, never falling along the last dimension, each value on 1 to 8 neighbouring positions
- offsets: int32 [16, 2], P('dp'), may hold values from 0 to 7
- gain_one: float32 [384], replicated, may hold values from 0.25 to 1.75
- qkv_one: bfloat16 [384, 1152], P(None, 'head'), may hold values from -0.3125 to 0.3125
- pools_one: float32 [3, 27, 96], replicated, may hold values from -1.25 to 1.25
- memory_one: float32 [2, 4, 96], replicated, may hold values from -3 to 3
- table_one: float32 [4, 15], P('head'), may hold values from -6 to 6
- proj_one: bfloat16 [384, 384], P('head'), may hold values from -0.3125 to 0.3125
- gain_two: float32 [384], replicated, may hold values from 0.25 to 1.75
- up_one: bfloat16 [384, 1536], P(None, 'head'), may hold values from -0.3125 to 0.3125
- down_one: bfloat16 [1536, 384], P('head'), may hold values from -0.15625 to 0.15625
- gain_three: float32 [384], replicated, may hold values from 0.25 to 1.75
- qkv_two: bfloat16 [384, 2304], P(None, 'head'), may hold values from -0.3125 to 0.3125
- residual_two: bfloat16 [384, 768], replicated, may hold values from -0.3125 to 0.3125
- pools_two: float32 [3, 27, 96], replicated, may hold values from -1.25 to 1.25
- memory_two: float32 [2, 4, 96], replicated, may hold values from -3 to 3
- table_two: float32 [8, 15], P('head'), may hold values from -6 to 6
- proj_two: bfloat16 [768, 768], P('head'), may hold values from -0.21875 to 0.21875
- gain_four: float32 [768], replicated, may hold values from 0.25 to 1.75
- up_two: bfloat16 [768, 3072], P(None, 'head'), may hold values from -0.21875 to 0.21875
- down_two: bfloat16 [3072, 768], P('head'), may hold values from -0.109375 to 0.109375
Outputs:
- blocks_out: bfloat16 [1600, 768], P(('dp', 'head'))
- grad_tokens: bfloat16 [6400, 384], P(('dp', 'head'))
- grad_gain_one: float32 [384], replicated
- grad_qkv_one: float32 [384, 1152], P(None, 'head')
- grad_pools_one: float32 [3, 27, 96], replicated
- grad_memory_one: float32 [2, 4, 96], replicated
- grad_table_one: float32 [4, 15], P('head')
- grad_proj_one: float32 [384, 384], P('head')
- grad_gain_two: float32 [384], replicated
- grad_up_one: float32 [384, 1536], P(None, 'head')
- grad_down_one: float32 [1536, 384], P('head')
- grad_gain_three: float32 [384], replicated
- grad_qkv_two: float32 [384, 2304], P(None, 'head')
- grad_residual_two: float32 [384, 768], replicated
- grad_pools_two: float32 [3, 27, 96], replicated
- grad_memory_two: float32 [2, 4, 96], replicated
- grad_table_two: float32 [8, 15], P('head')
- grad_proj_two: float32 [768, 768], P('head')
- grad_gain_four: float32 [768], replicated
- grad_up_two: float32 [768, 3072], P(None, 'head')
- grad_down_two: float32 [3072, 768], P('head')
Inputs may be any that keep to these rules, and one draw needn't show every extreme that they name: video_ids never falls along the clips; each video has 1 to 8 consecutive clips.
All inputs are finite; a program needn't handle non-finite values.
Results may differ from a plain program's by a relative error of at most 0.04.
Values may be sent and summed in bfloat16 or wider, within the bound.
No kernel may reach another device: no remote copies, remote signals or barrier semaphores. Data moves between devices by JAX's collectives and lax.ppermute only.
A program may use at most 256 MiB of HBM per device.

v0:
```python
import jax
import jax.numpy as jnp
from jax import lax
from jax.sharding import PartitionSpec as P

HD = 96
FR = 4
SIDE = 10


HIGH = lax.Precision.HIGHEST
EPSILON = 1e-06
NEGATIVE = -1e30


def passed_along(block, axis, distance):
    devices = range(lax.axis_size(axis))
    route = [(i - distance, i) for i in devices if i - distance in devices]
    return lax.ppermute(block, axis, route)


def layer_norm(values, gain):
    centered = values - jnp.mean(values, axis=-1, keepdims=True)
    variance = jnp.mean(centered * centered, axis=-1, keepdims=True)
    return centered * lax.rsqrt(variance + EPSILON) * gain


def pool_conv(fields, weight, stride):
    frames = fields.shape[1]
    side = fields.shape[2]
    padded = jnp.pad(fields, ((0, 0), (1, 1), (1, 1), (1, 1), (0, 0)))
    summed = jnp.zeros(
        (fields.shape[0], frames, side // stride, side // stride, fields.shape[4]), jnp.float32
    )
    for time_tap in range(3):
        for row_tap in range(3):
            for col_tap in range(3):
                tap_number = 9 * time_tap + 3 * row_tap + col_tap
                window = padded[
                    :,
                    time_tap : time_tap + frames,
                    row_tap : row_tap + side : stride,
                    col_tap : col_tap + side : stride,
                    :,
                ]
                summed = summed + window * weight[tap_number]
    return summed


def compress(fields, weight):
    clip_total = fields.shape[0]
    frames = fields.shape[1]
    side = fields.shape[2]
    grouped = fields.reshape(clip_total, frames // 4, 4, side * side, fields.shape[4])
    return jnp.sum(grouped * weight[None, None, :, None, :], axis=2).reshape(
        clip_total, frames // 4 * side * side, fields.shape[4]
    )


def shape_fields(projected, pools, memory, head_count, stride, key_stride):
    columns = projected.reshape(-1, FR, SIDE, SIDE, head_count, 3, HD)
    clip_total = columns.shape[0]
    channels = head_count * HD

    def take_field(which):
        return columns[:, :, :, :, :, which, :].reshape(clip_total, FR, SIDE, SIDE, channels)

    def tiled(kernel):
        return jnp.tile(kernel, (1, head_count))

    query_pool = pool_conv(take_field(0), tiled(pools[0]), stride)
    key_pool = pool_conv(take_field(1), tiled(pools[1]), key_stride)
    value_pool = pool_conv(take_field(2), tiled(pools[2]), key_stride)
    key_memory = compress(key_pool, tiled(memory[0]))
    value_memory = compress(value_pool, tiled(memory[1]))
    return (
        query_pool.reshape(clip_total, -1, channels),
        key_pool.reshape(clip_total, -1, channels),
        value_pool.reshape(clip_total, -1, channels),
        key_memory,
        value_memory,
    )


def relative_bias(table, pair, key_side):
    area = key_side * key_side
    quarter = FR // 4
    query_frame = lax.broadcasted_iota(jnp.int32, (FR, FR * area), 0)
    key_frame = lax.broadcasted_iota(jnp.int32, (FR, FR * area), 1) // area
    own_bins = query_frame - key_frame + FR - 1
    memory_frame = lax.broadcasted_iota(jnp.int32, (FR, quarter * area), 1) // area
    first_bins = 2 * FR - 1 + pair[0] * quarter + memory_frame
    second_bins = 2 * FR - 1 + pair[1] * quarter + memory_frame
    bin_index = jnp.concatenate([own_bins, first_bins, second_bins], 1)
    levels = lax.broadcasted_iota(jnp.int32, (1, 1, table.shape[1]), 2)
    onehot = (bin_index[:, :, None] == levels).astype(jnp.float32)
    return jnp.einsum("tkb,hb->htk", onehot, table, precision=HIGH)


def skip_pool(values):
    frames = values.shape[0] // (SIDE * SIDE)
    grid = values.reshape(frames, SIDE // 2, 2, SIDE // 2, 2, values.shape[1])
    return jnp.mean(grid, axis=(2, 4)).reshape(frames * (SIDE // 2) * (SIDE // 2), values.shape[1])


def spread(normed, weight):
    return jnp.dot(
        lax.all_gather(normed, "head", axis=0, tiled=True),
        weight,
        preferred_element_type=jnp.float32,
    )


def collect(values, weight):
    return lax.psum_scatter(
        jnp.dot(values, weight, preferred_element_type=jnp.float32).astype(jnp.bfloat16),
        "head",
        scatter_dimension=0,
        tiled=True,
    ).astype(jnp.float32)


def branch_back(grad_rows, kept, weight):
    piece = lax.all_gather(grad_rows, "head", axis=0, tiled=True)
    weight_sum = lax.dot_general(
        kept, piece, (((0,), (0,)), ((), ())), preferred_element_type=jnp.float32
    )
    rows_grad = lax.dot_general(
        piece, weight, (((1,), (1,)), ((), ())), preferred_element_type=jnp.float32
    )
    return (weight_sum, rows_grad)


def weight_grad(normed, grads):
    return lax.dot_general(
        lax.all_gather(normed, "head", axis=0, tiled=True),
        grads,
        (((0,), (0,)), ((), ())),
        preferred_element_type=jnp.float32,
    )


def input_grad(grads, weight):
    return lax.psum_scatter(
        lax.dot_general(
            grads, weight, (((1,), (1,)), ((), ())), preferred_element_type=jnp.float32
        ).astype(jnp.bfloat16),
        "head",
        scatter_dimension=0,
        tiled=True,
    ).astype(jnp.float32)


def scores_of(queries, keys_all, bias_grid, keep, head_count):
    rows = queries.shape[0]
    raw = jnp.einsum(
        "ihd,jhd->hij",
        queries.reshape(rows, head_count, HD),
        keys_all.reshape(-1, head_count, HD),
        preferred_element_type=jnp.float32,
    ) * HD ** (-0.5)
    raw = (raw.reshape(head_count, FR, rows // FR, -1) + bias_grid[:, :, None, :]).reshape(
        head_count, rows, -1
    )
    return jnp.where(keep[None, None, :], raw, NEGATIVE)


def attend(queries, keys_all, values_all, bias_grid, keep, head_count):
    rows = queries.shape[0]
    scores = scores_of(queries, keys_all, bias_grid, keep, head_count)
    top = jnp.max(scores, axis=-1, keepdims=True)
    weights = jnp.exp(scores - top)
    total = jnp.sum(weights, axis=-1, keepdims=True)
    probs = (weights / total).astype(jnp.bfloat16)
    mixture = jnp.einsum(
        "hij,jhd->ihd",
        probs,
        values_all.reshape(-1, head_count, HD),
        preferred_element_type=jnp.float32,
    )
    return (mixture.reshape(rows, -1), top + jnp.log(total))


def attend_back(queries, keys_all, values_all, bias_grid, keep, log_total, grad_mix, head_count):
    rows = queries.shape[0]
    scale = HD ** (-0.5)
    scores = scores_of(queries, keys_all, bias_grid, keep, head_count)
    probs = jnp.exp(scores - log_total)
    grad_heads = grad_mix.reshape(rows, head_count, HD)
    key_heads = keys_all.reshape(-1, head_count, HD)
    value_heads = values_all.reshape(-1, head_count, HD)
    query_heads = queries.reshape(rows, head_count, HD)
    grad_probs = jnp.einsum(
        "ihd,jhd->hij", grad_heads, value_heads, preferred_element_type=jnp.float32
    )
    inner = jnp.sum(grad_probs * probs, axis=-1, keepdims=True)
    grad_scores = (probs * (grad_probs - inner)).astype(jnp.bfloat16)
    query_grad = (
        jnp.einsum("hij,jhd->ihd", grad_scores, key_heads, preferred_element_type=jnp.float32)
        * scale
    )
    key_grad = (
        jnp.einsum("hij,ihd->jhd", grad_scores, query_heads, preferred_element_type=jnp.float32)
        * scale
    )
    value_grad = jnp.einsum(
        "hij,ihd->jhd", probs.astype(jnp.bfloat16), grad_heads, preferred_element_type=jnp.float32
    )
    bias_grad = jnp.sum(
        grad_scores.astype(jnp.float32).reshape(head_count, FR, rows // FR, -1), axis=2
    )
    return (
        query_grad.reshape(rows, -1),
        key_grad.reshape(key_heads.shape[0], -1),
        value_grad.reshape(value_heads.shape[0], -1),
        bias_grad,
    )


def block_forward(stream, weights, residual_weight, stride, key_stride, valids, offsets):
    (
        gain_first,
        qkv_weight,
        pools,
        memory,
        table,
        proj_weight,
        gain_second,
        up_weight,
        down_weight,
    ) = weights
    head_count = qkv_weight.shape[1] // (3 * HD)
    channels = head_count * HD
    clip_count = offsets.shape[0]
    key_side = SIDE // key_stride
    own_count = FR * key_side * key_side
    memory_count = FR // 4 * key_side * key_side
    keep_all = jnp.concatenate(
        [
            jnp.ones((clip_count, own_count), jnp.bool_),
            jnp.broadcast_to(valids[0][:, None], (clip_count, memory_count)),
            jnp.broadcast_to(valids[1][:, None], (clip_count, memory_count)),
        ],
        1,
    )
    normed = layer_norm(stream, gain_first).astype(jnp.bfloat16)
    projected = spread(normed, qkv_weight)
    query_pool, key_pool, value_pool, key_memory, value_memory = shape_fields(
        projected, pools, memory, head_count, stride, key_stride
    )
    key_low = key_memory.astype(jnp.bfloat16)
    value_low = value_memory.astype(jnp.bfloat16)
    prior_key, prior_value = passed_along((key_low, value_low), "dp", 1)
    key_ext = jnp.concatenate([prior_key, key_low], 0)
    value_ext = jnp.concatenate([prior_value, value_low], 0)
    keys_all = jnp.concatenate(
        [key_pool.astype(jnp.bfloat16), key_ext[1 : clip_count + 1], key_ext[:clip_count]], 1
    )
    values_all = jnp.concatenate(
        [value_pool.astype(jnp.bfloat16), value_ext[1 : clip_count + 1], value_ext[:clip_count]], 1
    )
    queries = query_pool.astype(jnp.bfloat16)
    bias_all = jax.vmap(lambda pair: relative_bias(table, pair, key_side))(offsets)

    def attend_clip(inputs):
        return attend(inputs[0], inputs[1], inputs[2], inputs[3], inputs[4], head_count)

    mixture, log_total = lax.map(attend_clip, (queries, keys_all, values_all, bias_all, keep_all))
    attention_rows = (mixture + query_pool).astype(jnp.bfloat16).reshape(-1, channels)
    branch = collect(attention_rows, proj_weight)
    if residual_weight is None:
        skip_linear = None
        middle = stream + branch
    else:
        skip_linear = jnp.dot(normed, residual_weight, preferred_element_type=jnp.float32)
        middle = skip_pool(skip_linear) + branch
    normed_mlp = layer_norm(middle, gain_second).astype(jnp.bfloat16)
    up_proj = spread(normed_mlp, up_weight)
    hidden = jax.nn.gelu(up_proj).astype(jnp.bfloat16)
    output = middle + collect(hidden, down_weight)
    kept = (
        stream,
        normed,
        projected,
        queries,
        keys_all,
        values_all,
        bias_all,
        log_total,
        attention_rows,
        skip_linear,
        middle,
        normed_mlp,
        up_proj,
        hidden,
        keep_all,
    )
    return (output, kept)


def block_backward(grad_output, kept, weights, residual_weight, stride, key_stride, offsets):
    (
        gain_first,
        qkv_weight,
        pools,
        memory,
        table,
        proj_weight,
        gain_second,
        up_weight,
        down_weight,
    ) = weights
    (
        stream,
        normed,
        projected,
        queries,
        keys_all,
        values_all,
        bias_all,
        log_total,
        attention_rows,
        skip_linear,
        middle,
        normed_mlp,
        up_proj,
        hidden,
        keep_all,
    ) = kept
    head_count = qkv_weight.shape[1] // (3 * HD)
    key_side = SIDE // key_stride
    own_count = FR * key_side * key_side
    memory_count = FR // 4 * key_side * key_side
    down_grad, hidden_grad = branch_back(grad_output.astype(jnp.bfloat16), hidden, down_weight)
    _, gelu_pull = jax.vjp(jax.nn.gelu, up_proj)
    up_grad = gelu_pull(hidden_grad)[0].astype(jnp.bfloat16)
    up_weight_grad = weight_grad(normed_mlp, up_grad)
    normed_mlp_grad = input_grad(up_grad, up_weight)
    _, second_pull = jax.vjp(layer_norm, middle, gain_second)
    middle_norm_grad, gain_second_grad = second_pull(normed_mlp_grad)
    middle_grad = grad_output + middle_norm_grad
    proj_grad, attention_grad = branch_back(
        middle_grad.astype(jnp.bfloat16), attention_rows, proj_weight
    )
    attention_low = attention_grad.astype(jnp.bfloat16).reshape(queries.shape)

    def clip_back(inputs):
        return attend_back(
            inputs[0], inputs[1], inputs[2], inputs[3], inputs[4], inputs[5], inputs[6], head_count
        )

    query_grad, keys_grad, values_grad, bias_grad = lax.map(
        clip_back, (queries, keys_all, values_all, bias_all, keep_all, log_total, attention_low)
    )

    def table_map(bias_table):
        return jax.vmap(lambda pair: relative_bias(bias_table, pair, key_side))(offsets)

    _, table_pull = jax.vjp(table_map, table)
    table_grad = table_pull(bias_grad)[0]
    query_pool_grad = query_grad + attention_low.astype(jnp.float32)
    edges = ((0, 0), (0, 0))
    first_end = own_count + memory_count
    key_ext_grad = jnp.pad(keys_grad[:, own_count:first_end], ((1, 1),) + edges) + jnp.pad(
        keys_grad[:, first_end:], ((0, 2),) + edges
    )
    value_ext_grad = jnp.pad(values_grad[:, own_count:first_end], ((1, 1),) + edges) + jnp.pad(
        values_grad[:, first_end:], ((0, 2),) + edges
    )
    later_key, later_value = (
        passed_along(key_ext_grad[:2].astype(jnp.bfloat16), "dp", -1).astype(jnp.float32),
        passed_along(value_ext_grad[:2].astype(jnp.bfloat16), "dp", -1).astype(jnp.float32),
    )
    key_memory_grad = key_ext_grad[2:] + later_key
    value_memory_grad = value_ext_grad[2:] + later_value

    def field_map(rows, pool_weights, memory_weights):
        return shape_fields(rows, pool_weights, memory_weights, head_count, stride, key_stride)

    _, field_pull = jax.vjp(field_map, projected, pools, memory)
    projected_grad, pools_grad, memory_grad = field_pull(
        (
            query_pool_grad,
            keys_grad[:, :own_count],
            values_grad[:, :own_count],
            key_memory_grad,
            value_memory_grad,
        )
    )
    projected_low = projected_grad.astype(jnp.bfloat16)
    qkv_grad = weight_grad(normed, projected_low)
    normed_grad = input_grad(projected_low, qkv_weight)
    if residual_weight is None:
        residual_grad = None
        stream_grad = middle_grad
    else:
        _, skip_pull = jax.vjp(skip_pool, skip_linear)
        linear_grad = skip_pull(middle_grad)[0].astype(jnp.bfloat16)
        residual_grad = lax.dot_general(
            normed, linear_grad, (((0,), (0,)), ((), ())), preferred_element_type=jnp.float32
        )
        normed_grad = normed_grad + lax.dot_general(
            linear_grad,
            residual_weight,
            (((1,), (1,)), ((), ())),
            preferred_element_type=jnp.float32,
        )
        stream_grad = jnp.zeros_like(stream)
    _, first_pull = jax.vjp(layer_norm, stream, gain_first)
    stream_norm_grad, gain_first_grad = first_pull(normed_grad)
    grads = (
        gain_first_grad,
        qkv_grad,
        pools_grad,
        memory_grad,
        table_grad,
        proj_grad,
        gain_second_grad,
        up_weight_grad,
        down_grad,
    )
    return (stream_grad + stream_norm_grad, grads, residual_grad)


def local(
    tokens,
    grad_out,
    video_ids,
    offsets,
    gain_one,
    qkv_one,
    pools_one,
    memory_one,
    table_one,
    proj_one,
    gain_two,
    up_one,
    down_one,
    gain_three,
    qkv_two,
    residual_two,
    pools_two,
    memory_two,
    table_two,
    proj_two,
    gain_four,
    up_two,
    down_two,
):
    clip_count = offsets.shape[0]
    first_clip = lax.axis_index("dp") * clip_count
    padded = jnp.concatenate([jnp.full((2,), -1, jnp.int32), video_ids])
    window = lax.dynamic_slice_in_dim(padded, first_clip, clip_count + 2)
    own_video = window[2:]
    valid_one = window[1 : clip_count + 1] == own_video
    valid_two = window[:clip_count] == own_video
    valids = (valid_one, valid_two)
    weights_first = (
        gain_one,
        qkv_one,
        pools_one,
        memory_one,
        table_one,
        proj_one,
        gain_two,
        up_one,
        down_one,
    )
    weights_second = (
        gain_three,
        qkv_two,
        pools_two,
        memory_two,
        table_two,
        proj_two,
        gain_four,
        up_two,
        down_two,
    )
    stream = tokens.astype(jnp.float32)
    middle_stream, kept_first = block_forward(stream, weights_first, None, 1, 2, valids, offsets)
    final, kept_second = block_forward(
        middle_stream, weights_second, residual_two, 2, 1, valids, offsets
    )
    middle_grad, grads_second, residual_grad = block_backward(
        grad_out.astype(jnp.float32), kept_second, weights_second, residual_two, 2, 1, offsets
    )
    tokens_grad, grads_first, unused = block_backward(
        middle_grad, kept_first, weights_first, None, 1, 2, offsets
    )
    summed = lax.psum(
        (
            grads_first[1],
            grads_first[4],
            grads_first[5],
            grads_first[7],
            grads_first[8],
            grads_second[1],
            grads_second[4],
            grads_second[5],
            grads_second[7],
            grads_second[8],
        ),
        "dp",
    )
    sums_first = summed[0:5]
    sums_second = summed[5:10]
    shared = lax.psum(
        (
            grads_first[0],
            grads_first[2],
            grads_first[3],
            grads_first[6],
            grads_second[0],
            residual_grad,
            grads_second[2],
            grads_second[3],
            grads_second[6],
        ),
        ("dp", "head"),
    )
    return (
        final.astype(jnp.bfloat16),
        tokens_grad.astype(jnp.bfloat16),
        shared[0],
        sums_first[0],
        shared[1],
        shared[2],
        sums_first[1],
        sums_first[2],
        shared[3],
        sums_first[3],
        sums_first[4],
        shared[4],
        sums_second[0],
        shared[5],
        shared[6],
        shared[7],
        sums_second[1],
        sums_second[2],
        shared[8],
        sums_second[3],
        sums_second[4],
    )


def solution(mesh):
    in_specs = (
        P(("dp", "head"), None),
        P(("dp", "head"), None),
        P(),
        P("dp", None),
        P(),
        P(None, "head"),
        P(),
        P(),
        P("head", None),
        P("head", None),
        P(),
        P(None, "head"),
        P("head", None),
        P(),
        P(None, "head"),
        P(),
        P(),
        P(),
        P("head", None),
        P("head", None),
        P(),
        P(None, "head"),
        P("head", None),
    )
    out_specs = (
        P(("dp", "head"), None),
        P(("dp", "head"), None),
        P(),
        P(None, "head"),
        P(),
        P(),
        P("head", None),
        P("head", None),
        P(),
        P(None, "head"),
        P("head", None),
        P(),
        P(None, "head"),
        P(),
        P(),
        P(),
        P("head", None),
        P("head", None),
        P(),
        P(None, "head"),
        P("head", None),
    )
    return jax.shard_map(local, mesh=mesh, in_specs=in_specs, out_specs=out_specs, check_vma=False)
```

profile of v0, /device:TPU:0, one launch (start us, length us, event | category | flops | bytes accessed | tf_op | source)
XLA Modules:
  0.0 2608.2 jit_solution(17611155937172573578)
XLA Ops:
  14.9 18.8 all_gather.28
  64.9 17.0 all-gather.1
  92.2 16.3 all_gather.29
  390.0 23.4 pad.1191
  413.5 23.3 pad.1190
  436.7 23.3 pad.1189
  460.0 23.3 pad.1188
  483.3 23.3 pad.1187
  506.6 23.4 pad.1186
  530.0 23.2 pad.1185
  553.2 23.3 pad.1184
  576.5 23.2 pad.1183
  599.7 23.3 pad.1182
  622.9 23.3 pad.1181
  646.2 23.3 pad.1180
  669.6 23.3 pad.1179
  692.9 23.2 pad.1178
  716.2 23.2 pad.1177
  739.4 23.3 pad.1176
  762.7 23.2 pad.1175
  785.9 23.2 pad.1174
  809.1 23.3 pad.1173
  832.4 23.3 pad.1171
  855.7 23.3 pad.1172
  878.9 23.1 pad.2785
  902.0 23.2 pad.2784
  925.2 16.3 pad.2783
  941.5 16.3 pad.2782
  957.8 16.3 pad.2781
  974.1 16.3 pad.2780
  990.4 19.1 add_add_fusion
  1102.5 20.9 reduce-scatter.26.cloned.1.call-done
  1125.8 16.9 all_gather.34
  1146.3 21.0 reduce-scatter.28.cloned.1.call-done
  1171.4 16.7 all_gather.35
  1223.3 22.8 pad.1253
  1246.1 22.8 pad.1252
  1269.0 22.7 pad.1251
  1291.7 22.7 pad.1250
  1330.4 22.7 pad.1248
  1353.1 22.7 pad.1247
  1391.7 22.7 pad.1245
  1414.4 22.6 pad.1244
  1437.0 16.1 pad.1243
  2225.4 16.1 all-reduce.367
  2242.5 75.4 %all-reduce.374.cloned.1.call-done = f32[384,768]{1,0:T(8,128)} async-done(((f32[384,768]{1,0:T(8,128)}), f32[384,768]{1,0:T(8,128)}) %all-reduce.374.cloned.1.call-update) | async-done | bytes 1179664 | tf_op jit(solution)/shard_map/psum | solution.py:508
  2317.9 133.0 %all-reduce.376.cloned.1.call-done = (f32[384]{0:T(512)}, f32[3,27,96]{2,1,0:T(8,128)}, f32[2,4,96]{2,1,0:T(4,128)}, f32[384]{0:T(512)}, f32[384]{0:T(512)}, /*i...) async-done(((f32[384]{0:T(512)}, f32[3,27,96]{2,1,0:T(8,128)}, f32[2,4,96]{2,1,0:T(4,128)}, f32[384]{0:T(512)}, f32[384]{0:T(512)}, ...) | async-done | bytes 76048 | tf_op jit(solution)/shard_map/psum | solution.py:508
  2450.9 131.3 %all-reduce.378.cloned.1.call-done = (f32[384,288]{0,1:T(8,128)}, f32[96,384]{1,0:T(8,128)}, f32[384,384]{1,0:T(8,128)}, f32[384,384]{1,0:T(8,128)}, f32[384,576...) async-done(((f32[384,288]{0,1:T(8,128)}, f32[96,384]{1,0:T(8,128)}, f32[384,384]{1,0:T(8,128)}, f32[384,384]{1,0:T(8,128)}, ...) | async-done | bytes 7962640 | tf_op jit(solution)/shard_map/psum | solution.py:491
  (1959 shorter events, 1314.2 us)
Async XLA Ops:
  7.2 316.2 %copy-start = (bf16[768,768]{1,0:T(8,128)(2,1)S(1)}, bf16[768,768]{1,0:T(8,128)(2,1)}, u32[]{:S(2)}) copy-start(bf16[768,768]{1,0:T(8,128)(2,1)} %param.52) | copy-start | bytes 3538948
  7.2 81.7 %reduce-scatter.22.cloned.1.call-start = ((), (), s32[]{:S(2)}) async-start(), calls=%async_computation.6 | async-start | bytes 768000
  10.2 34.9 %copy-start.416 = (f32[96]{0:T(128)}, f32[96]{0:T(128)S(1)}, u32[]{:S(2)}) copy-start(f32[96]{0:T(128)S(1)} %get-tuple-element.1226) | copy-start | bytes 1156
  40.6 18.3 collective-permute-start
  47.9 11.2 collective-permute-start.1
  57.3 73.9 %copy-start.238 = (f32[4,96]{1,0:T(4,128)}, f32[4,96]{1,0:T(4,128)S(1)}, u32[]{:S(2)}) copy-start(f32[4,96]{1,0:T(4,128)S(1)} %get-tuple-element.1253) | copy-start | bytes 4612
  57.3 110.0 %copy-start.236 = (f32[4,96]{1,0:T(4,128)}, f32[4,96]{1,0:T(4,128)S(1)}, u32[]{:S(2)}) copy-start(f32[4,96]{1,0:T(4,128)S(1)} %get-tuple-element.1252) | copy-start | bytes 4612
  64.8 44.6 %copy-start.143 = (bf16[384,384]{1,0:T(8,128)(2,1)S(1)}, bf16[384,384]{1,0:T(8,128)(2,1)}, u32[]{:S(2)}) copy-start(bf16[384,384]{1,0:T(8,128)(2,1)} %param.42) | copy-start | bytes 884740
  64.8 111.2 %reduce-scatter.24.cloned.1.call-start = ((), (), s32[]{:S(2)}) async-start(), calls=%async_computation.7 | async-start | bytes 768000
  112.6 55.5 %copy-start.591 = (u32[32]{0:T(128)S(1)}, u32[32]{0:T(128)}, u32[]{:S(2)}) copy-start(u32[32]{0:T(128)} %constant.951) | copy-start | bytes 388
  112.6 62.0 %copy-start.140 = (bf16[768,768]{1,0:T(8,128)(2,1)S(1)}, bf16[768,768]{1,0:T(8,128)(2,1)}, u32[]{:S(2)}) copy-start(bf16[768,768]{1,0:T(8,128)(2,1)} %param.53) | copy-start | bytes 3538948
  112.6 1010.8 %reduce-scatter.26.cloned.1.call-start = ((), (), s32[]{:S(2)}) async-start(), calls=%async_computation.8 | async-start | bytes 768000
  220.3 31.4 %collective-permute-start.2 = (bf16[2,100,192]{2,0,1:T(2,128)(2,1)}, bf16[2,100,192]{2,0,1:T(2,128)(2,1)}, u32[]{:S(2)}, u32[]{:S(2)}) collective-permute-start(bf16[2,100,192]{2,0,1:T(2,128)(2,1)} %bitcast.172), channel_id=1, source_target_pairs={{0,4},{4,8},{8,12},{12,16},{16,20},{20,24},{24,28},{1,5},{5,9},{9,... | collective-permute-start | bytes 230408 | tf_op jit(solution)/shard_map/ppermute | solution.py:19
  243.2 15.5 collective-permute-start.3
  295.8 5.4 collective-permute-start.8
  343.8 3.9 collective-permute-start.10
  345.3 4.2 collective-permute-start.9
  388.4 631.4 %copy-start.113 = (f32[2,100,192]{1,2,0:T(8,128)}, f32[2,100,192]{1,2,0:T(8,128)S(1)}, u32[]{:S(2)}) copy-start(f32[2,100,192]{1,2,0:T(8,128)S(1)} %get-tuple-element.915) | copy-start | bytes 460804
  388.5 633.7 %copy-start.18 = (f32[2,400,192]{1,2,0:T(8,128)}, f32[2,400,192]{1,2,0:T(8,128)S(1)}, u32[]{:S(2)}) copy-start(f32[2,400,192]{1,2,0:T(8,128)S(1)} %slice.2519) | copy-start | bytes 1843204
  389.0 634.4 %copy-start.111 = (f32[2,100,192]{1,2,0:T(8,128)}, f32[2,100,192]{1,2,0:T(8,128)S(1)}, u32[]{:S(2)}) copy-start(f32[2,100,192]{1,2,0:T(8,128)S(1)} %get-tuple-element.914) | copy-start | bytes 460804
  1020.5 7.3 collective-permute-start.5
  1024.1 20.9 collective-permute-start.4
  1099.4 67.9 %reduce-scatter.28.cloned.1.call-start = ((), (), s32[]{:S(2)}) async-start(), calls=%async_computation.9 | async-start | bytes 768000
  1125.7 44.5 %copy-start.42 = (f32[200,384]{1,0:T(8,128)}, f32[200,384]{1,0:T(8,128)S(1)}, u32[]{:S(2)}) copy-start(f32[200,384]{1,0:T(8,128)S(1)} %get-tuple-element.880) | copy-start | bytes 921604
  1125.7 44.5 %copy-start.246 = (f32[200]{0:T(256)}, f32[200]{0:T(256)S(1)}, u32[]{:S(2)}) copy-start(f32[200]{0:T(256)S(1)} %negate_multiply_fusion.2) | copy-start | bytes 2404
  1146.2 1073.0 %reduce-scatter.30.cloned.1.call-start = ((), (), s32[]{:S(2)}) async-start(), calls=%async_computation.10 | async-start | bytes 768000
  1146.2 42.7 %copy-start.205 = (bf16[96,384]{1,0:T(8,128)(2,1)S(1)}, bf16[96,384]{1,0:T(8,128)(2,1)}, u32[]{:S(2)}) copy-start(bf16[96,384]{1,0:T(8,128)(2,1)} %param.40) | copy-start | bytes 221188
  1207.9 7.4 collective-permute-start.7
  1209.2 10.3 collective-permute-start.6
  1269.0 45.4 %copy-start.185 = (f32[2,4,5,5,96]{4,1,3,2,0:T(4,128)S(1)}, f32[2,4,5,5,96]{4,1,3,2,0:T(4,128)}, u32[]{:S(2)}) copy-start(f32[2,4,5,5,96]{4,1,3,2,0:T(4,128)} %get-tuple-element.1072) | copy-start | bytes 230404
  1330.4 45.4 %copy-start.181 = (f32[2,4,5,5,96]{4,1,3,2,0:T(4,128)S(1)}, f32[2,4,5,5,96]{4,1,3,2,0:T(4,128)}, u32[]{:S(2)}) copy-start(f32[2,4,5,5,96]{4,1,3,2,0:T(4,128)} %get-tuple-element.1075) | copy-start | bytes 230404
  1391.7 45.3 %copy-start.180 = (f32[2,4,5,5,96]{4,1,3,2,0:T(4,128)S(1)}, f32[2,4,5,5,96]{4,1,3,2,0:T(4,128)}, u32[]{:S(2)}) copy-start(f32[2,4,5,5,96]{4,1,3,2,0:T(4,128)} %get-tuple-element.1078) | copy-start | bytes 230404
  1564.9 32.0 %copy-start.179 = (f32[2,4,5,5,96]{4,1,3,2,0:T(4,128)S(1)}, f32[2,4,5,5,96]{4,1,3,2,0:T(4,128)}, u32[]{:S(2)}) copy-start(f32[2,4,5,5,96]{4,1,3,2,0:T(4,128)} %get-tuple-element.1061) | copy-start | bytes 230404
  1580.9 32.0 %copy-start.178 = (f32[2,4,5,5,96]{4,1,3,2,0:T(4,128)S(1)}, f32[2,4,5,5,96]{4,1,3,2,0:T(4,128)}, u32[]{:S(2)}) copy-start(f32[2,4,5,5,96]{4,1,3,2,0:T(4,128)} %get-tuple-element.1067) | copy-start | bytes 230404
  1692.9 32.0 %copy-start.197 = (f32[2,4,5,5,96]{4,1,3,2,0:T(4,128)S(1)}, f32[2,4,5,5,96]{4,1,3,2,0:T(4,128)}, u32[]{:S(2)}) copy-start(f32[2,4,5,5,96]{4,1,3,2,0:T(4,128)} %get-tuple-element.1043) | copy-start | bytes 230404
  1724.8 32.0 %copy-start.195 = (f32[2,4,5,5,96]{4,1,3,2,0:T(4,128)S(1)}, f32[2,4,5,5,96]{4,1,3,2,0:T(4,128)}, u32[]{:S(2)}) copy-start(f32[2,4,5,5,96]{4,1,3,2,0:T(4,128)} %get-tuple-element.1045) | copy-start | bytes 230404
  1740.8 32.0 %copy-start.194 = (f32[2,4,5,5,96]{4,1,3,2,0:T(4,128)S(1)}, f32[2,4,5,5,96]{4,1,3,2,0:T(4,128)}, u32[]{:S(2)}) copy-start(f32[2,4,5,5,96]{4,1,3,2,0:T(4,128)} %get-tuple-element.1046) | copy-start | bytes 230404
  1756.8 32.0 %copy-start.193 = (f32[2,4,5,5,96]{4,1,3,2,0:T(4,128)S(1)}, f32[2,4,5,5,96]{4,1,3,2,0:T(4,128)}, u32[]{:S(2)}) copy-start(f32[2,4,5,5,96]{4,1,3,2,0:T(4,128)} %get-tuple-element.1047) | copy-start | bytes 230404
  1772.8 32.0 %copy-start.192 = (f32[2,4,5,5,96]{4,1,3,2,0:T(4,128)S(1)}, f32[2,4,5,5,96]{4,1,3,2,0:T(4,128)}, u32[]{:S(2)}) copy-start(f32[2,4,5,5,96]{4,1,3,2,0:T(4,128)} %get-tuple-element.1048) | copy-start | bytes 230404
  1836.6 31.9 %copy-start.177 = (f32[2,4,5,5,96]{4,1,3,2,0:T(4,128)S(1)}, f32[2,4,5,5,96]{4,1,3,2,0:T(4,128)}, u32[]{:S(2)}) copy-start(f32[2,4,5,5,96]{4,1,3,2,0:T(4,128)} %get-tuple-element.1053) | copy-start | bytes 230404
  1884.6 32.0 %copy-start.174 = (f32[2,4,5,5,96]{4,1,3,2,0:T(4,128)S(1)}, f32[2,4,5,5,96]{4,1,3,2,0:T(4,128)}, u32[]{:S(2)}) copy-start(f32[2,4,5,5,96]{4,1,3,2,0:T(4,128)} %get-tuple-element.1056) | copy-start | bytes 230404
  1900.5 32.0 %copy-start.173 = (f32[2,4,5,5,96]{4,1,3,2,0:T(4,128)S(1)}, f32[2,4,5,5,96]{4,1,3,2,0:T(4,128)}, u32[]{:S(2)}) copy-start(f32[2,4,5,5,96]{4,1,3,2,0:T(4,128)} %get-tuple-element.1057) | copy-start | bytes 230404
  1980.3 31.9 %copy-start.188 = (f32[2,4,5,5,96]{4,1,3,2,0:T(4,128)S(1)}, f32[2,4,5,5,96]{4,1,3,2,0:T(4,128)}, u32[]{:S(2)}) copy-start(f32[2,4,5,5,96]{4,1,3,2,0:T(4,128)} %get-tuple-element.1034) | copy-start | bytes 230404
  2028.2 47.6 %copy-start.183 = (f32[2,4,5,5,96]{4,1,3,2,0:T(4,128)S(1)}, f32[2,4,5,5,96]{4,1,3,2,0:T(4,128)}, u32[]{:S(2)}) copy-start(f32[2,4,5,5,96]{4,1,3,2,0:T(4,128)} %get-tuple-element.1037) | copy-start | bytes 230404
  2159.3 158.6 %all-reduce.374.cloned.1.call-start = ((), (), s32[]{:S(2)}) async-start(), calls=%async_computation.5 | async-start | bytes 2359296 | tf_op jit(solution)/shard_map/psum | solution.py:508
  2178.3 272.7 %all-reduce.376.cloned.1.call-start = ((), (), s32[]{:S(2)}) async-start(), calls=%async_computation.11 | async-start | bytes 233472 | tf_op jit(solution)/shard_map/psum | solution.py:508
  2222.1 360.1 %all-reduce.378.cloned.1.call-start = ((), (), s32[]{:S(2)}) async-start(), calls=%async_computation.12 | async-start | bytes 15925248 | tf_op jit(solution)/shard_map/psum | solution.py:491
  2450.9 138.8 %copy-start.563 = (f32[384]{0:T(512)S(1)}, f32[384]{0:T(512)}, u32[]{:S(2)}) copy-start(f32[384]{0:T(512)} %get-tuple-element.1689) | copy-start | bytes 4612
  (606 other events, 4517.8 us)
Sparse Core Ops, SparseCore 0:
  64.9 23.9 reduce-scatter.21
  112.7 21.5 reduce-scatter.23
  1099.5 23.8 reduce-scatter.25
  1146.3 20.9 reduce-scatter.27
  2159.4 23.0 reduce-scatter.29
  2188.3 129.5 all-reduce.373
  2327.2 123.7 all-reduce.375
  2457.5 124.7 all-reduce.377
where the time goes:
time: 2660 us; the launch traced here: 2610 us
  local copies, waits for them, and re-layouts  1720 us (65%)
  waiting for transfers between devices  387 us (15%)
  other arithmetic  225 us (8%)
  blocking collectives  179 us (7%)
  matrix products  52.5 us (2%)
    pad x63, local copies, waits for them, and re-layouts, pool_conv(): padded[:, time_tap:time_tap + frames, row_tap:row_tap + side:stride, col_...  1210 us
    unnamed x1247, local copies, waits for them, and re-layouts  329 us
    psum x2, waiting for transfers between devices, local(): lax.psum((grads_first[0], grads_first[2], grads_first[3], grads_first[6],...  208 us
    psum x1, waiting for transfers between devices, local(): lax.psum((grads_first[1], grads_first[4], grads_first[5], grads_first[7],...  131 us
    add_any x9, other arithmetic, pool_conv(): padded[:, time_tap:time_tap + frames, row_tap:row_tap + side:stride, col_...  66.9 us
    all_gather x4, blocking collectives, spread(): lax.all_gather(normed, 'head', axis=0, tiled=True)  65.5 us
    all_gather x4, blocking collectives, branch_back(): piece = lax.all_gather(grad_rows, 'head', axis=0, tiled=True)  65.4 us
    another operation x167, local copies, waits for them, and re-layouts, tiled(): return jnp.tile(kernel, (1, head_count))  54.1 us
  transfers between devices with their start and end apart: 19, of which 6 were waited for; matrix products, arithmetic and copies ran while one was open for 8% of the time, Pallas kernels for 0%

commit v1 on v0

--- a/solution.py
+++ b/solution.py
@@ -29,9 +29,7 @@
     frames = fields.shape[1]
     side = fields.shape[2]
     padded = jnp.pad(fields, ((0, 0), (1, 1), (1, 1), (1, 1), (0, 0)))
-    summed = jnp.zeros(
-        (fields.shape[0], frames, side // stride, side // stride, fields.shape[4]), jnp.float32
-    )
+    summed = jnp.zeros(fields.shape, jnp.float32)
     for time_tap in range(3):
         for row_tap in range(3):
             for col_tap in range(3):
@@ -39,11 +37,17 @@
                 window = padded[
                     :,
                     time_tap : time_tap + frames,
-                    row_tap : row_tap + side : stride,
-                    col_tap : col_tap + side : stride,
+                    row_tap : row_tap + side,
+                    col_tap : col_tap + side,
                     :,
                 ]
                 summed = summed + window * weight[tap_number]
+    if stride > 1:
+        small = side // stride
+        grid = summed.reshape(
+            fields.shape[0], frames, small, stride, small, stride, fields.shape[4]
+        )
+        summed = grid[:, :, :, 0, :, 0, :]
     return summed
 
 

time: 2660 us -> 1090 us (0.41); the launches traced: 2610 us -> 1080 us
  local copies, waits for them, and re-layouts: 1720 us -> 201 us
    pad x63 -> x5, local copies, waits for them, and re-layouts: 1210 us -> 1.89 us  [pool_conv(): summed = grid[:, :, :, 0, :, 0, :]]
    unnamed x1247 -> x899, local copies, waits for them, and re-layouts: 329 us -> 38.1 us
    add_any x9, other arithmetic: 66.9 us -> 32.7 us  [pool_conv(): padded[:, time_tap:time_tap + frames, row_tap:row_tap + side, col_tap:col...]
  transfers between devices with their start and end apart: 19 -> 19, of which waited for: 6 -> 7; matrix products, arithmetic and copies ran while one was open for 8% -> 21% of each run, Pallas kernels for 0% -> 0%
where the time goes in v1:
time: 1090 us; the launch traced here: 1080 us
  waiting for transfers between devices  379 us (35%)
  other arithmetic  209 us (19%)
  local copies, waits for them, and re-layouts  201 us (18%)
  blocking collectives  179 us (16%)
  matrix products  56.6 us (5%)
  starting transfers between devices  32.1 us (3%)
  between operations  21.8 us (2%)
    psum x2, waiting for transfers between devices, local(): lax.psum((grads_first[0], grads_first[2], grads_first[3], grads_first[6],...  201 us
    psum x1, waiting for transfers between devices, local(): lax.psum((grads_first[1], grads_first[4], grads_first[5], grads_first[7],...  131 us
    all_gather x4, blocking collectives, spread(): lax.all_gather(normed, 'head', axis=0, tiled=True)  65.4 us
    all_gather x4, blocking collectives, branch_back(): piece = lax.all_gather(grad_rows, 'head', axis=0, tiled=True)  65.3 us
    reduce_sum x13, other arithmetic, pool_conv(): summed = summed + window * weight[tap_number]  60.1 us
    another operation x167, local copies, waits for them, and re-layouts, tiled(): return jnp.tile(kernel, (1, head_count))  52.5 us
    unnamed x16, waiting for transfers between devices  46.4 us
    unnamed x899, local copies, waits for them, and re-layouts  38.1 us
  transfers between devices with their start and end apart: 19, of which 7 were waited for; matrix products, arithmetic and copies ran while one was open for 21% of the time, Pallas kernels for 0%

profile of v1, /device:TPU:0, one launch (start us, length us, event | category | flops | bytes accessed | tf_op | source)
XLA Modules:
  0.0 1078.8 jit_solution(1959536313522271548)
XLA Ops:
  17.8 18.8 %all_gather.28 = bf16[800,384]{1,0:T(8,128)(2,1)S(1)} all-gather(bf16[200,384]{1,0:T(8,128)(2,1)S(1)} %fusion.90), channel_id=1, replica_groups=mesh['dp'=8,'head'=4] {'head'}, dimensions={0}, use_global_device_ids=true | all-gather | bytes 768000 | tf_op jit(solution)/shard_map/all_gather | solution.py:112
  42.9 3.5 multiply_add_fusion.3
  48.9 3.5 multiply_add_fusion.5
  52.7 4.3 collective-permute-start
  57.1 3.6 multiply_add_fusion.4
  69.1 17.4 %all-gather.1 = bf16[4,50,768]{2,1,0:T(8,128)(2,1)S(1)} all-gather(bf16[1,50,768]{2,1,0:T(8,128)(2,1)S(1)} %bitcast.954), channel_id=1, replica_groups=mesh['dp'=8,'head'=4] {'head'}, dimensions={0}, use_global_device_ids=true | all-gather | bytes 384000 | tf_op jit(solution)/shard_map/all_gather | solution.py:128
  86.7 6.4 reduce-scatter.22.cloned.1.call-done
  96.3 15.8 %all_gather.29 = bf16[800,384]{1,0:T(8,128)(2,1)S(1)} all-gather(bf16[200,384]{1,0:T(8,128)(2,1)S(1)} %multiply_convert_fusion.5), channel_id=1, replica_groups=mesh['dp'=8,'head'=4] {'head'}, dimensions={0}, use_global_device_ids=true | all-gather | bytes 768000 | tf_op jit(solution)/shard_map/all_gather | solution.py:112
  174.8 15.8 %all_gather.30 = bf16[800,384]{1,0:T(8,128)(2,1)S(1)} all-gather(bf16[200,384]{1,0:T(8,128)(2,1)S(1)} %multiply_convert_fusion.4), channel_id=1, replica_groups=mesh['dp'=8,'head'=4] {'head'}, dimensions={0}, use_global_device_ids=true | all-gather | bytes 768000 | tf_op jit(solution)/shard_map/all_gather | solution.py:112
  192.7 5.2 reshape.2417
  198.0 7.7 fusion.147
  206.6 7.3 fusion.142
  220.2 7.6 fusion.143
  229.1 12.6 %collective-permute-start.2 = (bf16[2,100,192]{2,0,1:T(2,128)(2,1)}, bf16[2,100,192]{2,0,1:T(2,128)(2,1)}, u32[]{:S(2)}, u32[]{:S(2)}) collective-permute-start(bf16[2,100,192]{2,0,1:T(2,128)(2,1)} %bitcast.174), channel_id=1, source_target_pairs={{0,4},{4,8},{8,12},{12,16},{16,20},{20,24},{24,28},{1,5},{5,9},{9,... | collective-permute-start | bytes 230408 | tf_op jit(solution)/shard_map/ppermute | solution.py:19
  244.8 6.8 multiply_add_fusion.1
  260.2 5.6 fusion.74
  267.3 5.4 fusion.76
  274.9 5.9 while.57
  286.3 16.3 %fusion = bf16[56,768]{1,0:T(8,128)(2,1)} fusion(bf16[200,768]{1,0:T(8,128)(2,1)} %convolution_convert_fusion.7), kind=kCustom, calls=%all-reduce-scatter | all-reduce-scatter fusion | flops 172033 | bytes 393728
  314.7 15.0 %all-gather = bf16[4,50,768]{2,1,0:T(8,128)(2,1)} all-gather(bf16[1,50,768]{2,1,0:T(8,128)(2,1)S(1)} %fusion.113), channel_id=1, replica_groups=mesh['dp'=8,'head'=4] {'head'}, dimensions={0}, use_global_device_ids=true | all-gather | bytes 384000 | tf_op jit(solution)/shard_map/all_gather | solution.py:112
  336.1 15.5 %fusion.138 = (bf16[56,768]{1,0:T(8,128)(2,1)S(1)}, bf16[56,768]{1,0:T(8,128)(2,1)S(1)}) fusion(bf16[200,768]{1,0:T(8,128)(2,1)S(1)} %convolution_convert_fusion.6, bf16[200,768]{1,0:T(8,128)(2,1)S(1)} %copy-done.140), kind=kCustom, calls=%all-reduce-scatter.3 | all-reduce-scatter fusion | flops 344065 | bytes 786944
  359.1 14.5 %all-gather.2 = bf16[4,50,768]{2,1,0:T(8,128)(2,1)S(1)} all-gather(bf16[1,50,768]{2,1,0:T(8,128)(2,1)S(1)} %get-tuple-element.1075), channel_id=1, replica_groups=mesh['dp'=8,'head'=4] {'head'}, dimensions={0}, use_global_device_ids=true | all-gather | bytes 384000 | tf_op jit(solution)/shard_map/all_gather | solution.py:128
  375.5 13.1 %while.58 = (s32[]{:T(128)}, f32[2,100,192]{1,2,0:T(8,128)}, f32[2,600,192]{1,2,0:T(8,128)}, f32[2,600,192]{1,2,0:T(8,128)}, f32[2,2,4,600]{3,1,2,0:T(2,128)}, /...) while((s32[]{:T(128)}, f32[2,100,192]{1,2,0:T(8,128)}, ...), condition=%wide.region_31.32_spmd, body=%wide.region_28.31_spmd.sunk | while | flops 116649400 | bytes 25996796 | solution.py:356
  394.2 4.7 multiply_reduce_fusion.29
  402.5 5.3 pad_add_fusion
  418.5 5.1 multiply_reduce_fusion.83
  423.8 5.7 broadcast_multiply_fusion.54
  435.0 5.1 multiply_reduce_fusion.56
  440.4 7.5 broadcast_multiply_fusion
  448.1 4.7 broadcast_multiply_fusion.1
  454.1 5.3 pad_add_fusion.2
  462.3 8.4 pad_add_fusion.1
  481.0 4.1 convert_element_type.310
  490.0 22.2 %reduce-scatter.26.cloned.1.call-done = bf16[200,384]{1,0:T(8,128)(2,1)} async-done(((bf16[800,384]{1,0:T(8,128)(2,1)}), bf16[200,384]{1,0:T(8,128)(2,1)}) %reduce-scatter.26.cloned.1.call-update) | async-done | bytes 153616
  514.6 16.7 %all_gather.34 = bf16[800,384]{1,0:T(8,128)(2,1)S(1)} all-gather(bf16[200,384]{1,0:T(8,128)(2,1)S(1)} %add_convert_fusion.4), channel_id=1, replica_groups=mesh['dp'=8,'head'=4] {'head'}, dimensions={0}, use_global_device_ids=true | all-gather | bytes 768000 | tf_op jit(solution)/shard_map/all_gather | solution.py:128
  539.6 17.0 %reduce-scatter.28.cloned.1.call-done = bf16[200,384]{1,0:T(8,128)(2,1)} async-done(((bf16[800,384]{1,0:T(8,128)(2,1)}), bf16[200,384]{1,0:T(8,128)(2,1)}) %reduce-scatter.28.cloned.1.call-update) | async-done | bytes 153616
  560.7 16.7 %all_gather.35 = bf16[800,384]{1,0:T(8,128)(2,1)S(1)} all-gather(bf16[200,384]{1,0:T(8,128)(2,1)S(1)} %fusion.134), channel_id=1, replica_groups=mesh['dp'=8,'head'=4] {'head'}, dimensions={0}, use_global_device_ids=true | all-gather | bytes 768000 | tf_op jit(solution)/shard_map/all_gather | solution.py:128
  580.5 10.8 while.59
  609.0 3.5 multiply_reduce_fusion.166
  636.1 3.7 reshape.2442
  645.3 6.3 multiply_reduce_fusion.30
  656.6 5.6 multiply_reduce_fusion.84
  662.2 6.4 multiply_reduce_fusion.57
  670.3 8.5 multiply_reduce_fusion.71
  703.4 16.4 %all-reduce.370 = (f32[1,15]{1,0:T(1,128)}, f32[2,15]{1,0:T(2,128)}) all-reduce(f32[1,15]{1,0:T(1,128)S(1)} %convolution_bitcast_fusion.4, f32[2,15]{1,0:T(2,128)S(1)} %convolution_bitcast_fusion.3), channel_id=1, replica_groups=mesh['dp'=8,'head'=4] {'dp'}, use_global_device_ids=true, to_apply=%region_133.134 | all-reduce | flops 45 | bytes 360 | tf_op jit(solution)/shard_map/psum | solution.py:495
  720.8 67.8 %all-reduce.377.cloned.1.call-done = f32[384,768]{1,0:T(8,128)} async-done(((f32[384,768]{1,0:T(8,128)}), f32[384,768]{1,0:T(8,128)}) %all-reduce.377.cloned.1.call-update) | async-done | bytes 1179664 | tf_op jit(solution)/shard_map/psum | solution.py:512
  788.6 133.0 %all-reduce.379.cloned.1.call-done = (f32[384]{0:T(512)}, f32[3,27,96]{2,1,0:T(8,128)}, f32[2,4,96]{2,1,0:T(4,128)}, f32[384]{0:T(512)}, f32[384]{0:T(512)}, /*i...) async-done(((f32[384]{0:T(512)}, f32[3,27,96]{2,1,0:T(8,128)}, f32[2,4,96]{2,1,0:T(4,128)}, f32[384]{0:T(512)}, f32[384]{0:T(512)}, ...) | async-done | bytes 76048 | tf_op jit(solution)/shard_map/psum | solution.py:512
  921.6 131.3 %all-reduce.381.cloned.1.call-done = (f32[384,288]{0,1:T(8,128)}, f32[96,384]{1,0:T(8,128)}, f32[384,384]{1,0:T(8,128)}, f32[384,384]{1,0:T(8,128)}, f32[384,576...) async-done(((f32[384,288]{0,1:T(8,128)}, f32[96,384]{1,0:T(8,128)}, f32[384,384]{1,0:T(8,128)}, f32[384,384]{1,0:T(8,128)}, ...) | async-done | bytes 7962640 | tf_op jit(solution)/shard_map/psum | solution.py:495
  (1520 shorter events, 340.2 us)
Async XLA Ops:
  7.2 324.3 %copy-start = (bf16[768,768]{1,0:T(8,128)(2,1)S(1)}, bf16[768,768]{1,0:T(8,128)(2,1)}, u32[]{:S(2)}) copy-start(bf16[768,768]{1,0:T(8,128)(2,1)} %param.52) | copy-start | bytes 3538948
  7.2 85.8 %reduce-scatter.22.cloned.1.call-start = ((), (), s32[]{:S(2)}) async-start(), calls=%async_computation.6 | async-start | bytes 768000
  8.8 33.9 %copy-start.312 = (f32[96]{0:T(128)}, f32[96]{0:T(128)S(1)}, u32[]{:S(2)}) copy-start(f32[96]{0:T(128)S(1)} %get-tuple-element.1166) | copy-start | bytes 1156
  8.8 33.9 %copy-start.314 = (f32[96]{0:T(128)}, f32[96]{0:T(128)S(1)}, u32[]{:S(2)}) copy-start(f32[96]{0:T(128)S(1)} %get-tuple-element.1167) | copy-start | bytes 1156
  8.8 33.9 %copy-start.316 = (f32[96]{0:T(128)}, f32[96]{0:T(128)S(1)}, u32[]{:S(2)}) copy-start(f32[96]{0:T(128)S(1)} %get-tuple-element.1168) | copy-start | bytes 1156
  8.8 33.9 %copy-start.318 = (f32[96]{0:T(128)}, f32[96]{0:T(128)S(1)}, u32[]{:S(2)}) copy-start(f32[96]{0:T(128)S(1)} %get-tuple-element.1169) | copy-start | bytes 1156
  8.9 33.9 %copy-start.320 = (f32[96]{0:T(128)}, f32[96]{0:T(128)S(1)}, u32[]{:S(2)}) copy-start(f32[96]{0:T(128)S(1)} %get-tuple-element.1170) | copy-start | bytes 1156
  8.9 33.9 %copy-start.322 = (f32[96]{0:T(128)}, f32[96]{0:T(128)S(1)}, u32[]{:S(2)}) copy-start(f32[96]{0:T(128)S(1)} %get-tuple-element.1171) | copy-start | bytes 1156
  8.9 33.9 %copy-start.324 = (f32[96]{0:T(128)}, f32[96]{0:T(128)S(1)}, u32[]{:S(2)}) copy-start(f32[96]{0:T(128)S(1)} %get-tuple-element.1172) | copy-start | bytes 1156
  8.9 33.9 %copy-start.326 = (f32[96]{0:T(128)}, f32[96]{0:T(128)S(1)}, u32[]{:S(2)}) copy-start(f32[96]{0:T(128)S(1)} %get-tuple-element.1173) | copy-start | bytes 1156
  12.3 36.6 %copy-start.344 = (f32[96]{0:T(128)}, f32[96]{0:T(128)S(1)}, u32[]{:S(2)}) copy-start(f32[96]{0:T(128)S(1)} %get-tuple-element.1216) | copy-start | bytes 1156
  12.3 36.6 %copy-start.346 = (f32[96]{0:T(128)}, f32[96]{0:T(128)S(1)}, u32[]{:S(2)}) copy-start(f32[96]{0:T(128)S(1)} %get-tuple-element.1217) | copy-start | bytes 1156
  12.3 36.6 %copy-start.348 = (f32[96]{0:T(128)}, f32[96]{0:T(128)S(1)}, u32[]{:S(2)}) copy-start(f32[96]{0:T(128)S(1)} %get-tuple-element.1218) | copy-start | bytes 1156
  12.3 36.6 %copy-start.350 = (f32[96]{0:T(128)}, f32[96]{0:T(128)S(1)}, u32[]{:S(2)}) copy-start(f32[96]{0:T(128)S(1)} %get-tuple-element.1219) | copy-start | bytes 1156
  14.0 34.9 %copy-start.352 = (f32[96]{0:T(128)}, f32[96]{0:T(128)S(1)}, u32[]{:S(2)}) copy-start(f32[96]{0:T(128)S(1)} %get-tuple-element.1221) | copy-start | bytes 1156
  14.0 34.9 %copy-start.354 = (f32[96]{0:T(128)}, f32[96]{0:T(128)S(1)}, u32[]{:S(2)}) copy-start(f32[96]{0:T(128)S(1)} %get-tuple-element.1222) | copy-start | bytes 1156
  14.0 34.9 %copy-start.356 = (f32[96]{0:T(128)}, f32[96]{0:T(128)S(1)}, u32[]{:S(2)}) copy-start(f32[96]{0:T(128)S(1)} %get-tuple-element.1223) | copy-start | bytes 1156
  14.0 34.9 %copy-start.358 = (f32[96]{0:T(128)}, f32[96]{0:T(128)S(1)}, u32[]{:S(2)}) copy-start(f32[96]{0:T(128)S(1)} %get-tuple-element.1224) | copy-start | bytes 1156
  46.5 16.7 %collective-permute-start.1 = (bf16[2,25,96]{2,0,1:T(2,128)(2,1)S(1)}, bf16[2,25,96]{2,0,1:T(2,128)(2,1)S(1)}, u32[]{:S(2)}, u32[]{:S(2)}) collective-permute-start(bf16[2,25,96]{2,0,1:T(2,128)(2,1)S(1)} %bitcast.965), channel_id=1, source_target_pairs={{0,4},{4,8},{8,12},{12,16},{16,20},{20,24},{24,28},{1,5},{5,9},{9,... | collective-permute-start | bytes 28808 | tf_op jit(solution)/shard_map/ppermute | solution.py:19
  52.7 10.7 collective-permute-start
  61.5 72.4 %copy-start.201 = (f32[4,96]{1,0:T(4,128)}, f32[4,96]{1,0:T(4,128)S(1)}, u32[]{:S(2)}) copy-start(f32[4,96]{1,0:T(4,128)S(1)} %get-tuple-element.1248) | copy-start | bytes 4612
  61.5 89.9 %copy-start.203 = (f32[4,96]{1,0:T(4,128)}, f32[4,96]{1,0:T(4,128)S(1)}, u32[]{:S(2)}) copy-start(f32[4,96]{1,0:T(4,128)S(1)} %get-tuple-element.1249) | copy-start | bytes 4612
  69.0 43.9 %copy-start.149 = (bf16[384,384]{1,0:T(8,128)(2,1)S(1)}, bf16[384,384]{1,0:T(8,128)(2,1)}, u32[]{:S(2)}) copy-start(bf16[384,384]{1,0:T(8,128)(2,1)} %param.42) | copy-start | bytes 884740
  69.1 104.2 %reduce-scatter.24.cloned.1.call-start = ((), (), s32[]{:S(2)}) async-start(), calls=%async_computation.7 | async-start | bytes 768000
  116.0 52.8 %copy-start.434 = (u32[32]{0:T(128)S(1)}, u32[32]{0:T(128)}, u32[]{:S(2)}) copy-start(u32[32]{0:T(128)} %constant.957) | copy-start | bytes 388
  116.0 54.4 %copy-start.440 = (f32[2,15]{1,0:T(2,128)S(1)}, f32[2,15]{1,0:T(2,128)}, u32[]{:S(2)}) copy-start(f32[2,15]{1,0:T(2,128)} %param.49) | copy-start | bytes 364
  116.0 396.2 %reduce-scatter.26.cloned.1.call-start = ((), (), s32[]{:S(2)}) async-start(), calls=%async_computation.8 | async-start | bytes 768000
  134.0 79.9 %copy-start.183 = (f32[4,192]{1,0:T(4,128)}, f32[4,192]{1,0:T(4,128)S(1)}, u32[]{:S(2)}) copy-start(f32[4,192]{1,0:T(4,128)S(1)} %tile.541) | copy-start | bytes 9220
  151.5 76.3 %copy-start.185 = (f32[4,192]{1,0:T(4,128)}, f32[4,192]{1,0:T(4,128)S(1)}, u32[]{:S(2)}) copy-start(f32[4,192]{1,0:T(4,128)S(1)} %tile.430) | copy-start | bytes 9220
  174.8 77.0 %copy-start.109 = (bf16[200,384]{1,0:T(8,128)(2,1)}, bf16[200,384]{1,0:T(8,128)(2,1)S(1)}, u32[]{:S(2)}) copy-start(bf16[200,384]{1,0:T(8,128)(2,1)S(1)} %multiply_convert_fusion.4) | copy-start | bytes 460804
  215.2 45.0 %collective-permute-start.3 = (bf16[2,100,192]{2,0,1:T(2,128)(2,1)}, bf16[2,100,192]{2,0,1:T(2,128)(2,1)}, u32[]{:S(2)}, u32[]{:S(2)}) collective-permute-start(bf16[2,100,192]{2,0,1:T(2,128)(2,1)} %bitcast.233), channel_id=1, source_target_pairs={{0,4},{4,8},{8,12},{12,16},{16,20},{20,24},{24,28},{1,5},{5,9},{9,... | collective-permute-start | bytes 230408 | tf_op jit(solution)/shard_map/ppermute | solution.py:19
  229.1 38.2 %collective-permute-start.2 = (bf16[2,100,192]{2,0,1:T(2,128)(2,1)}, bf16[2,100,192]{2,0,1:T(2,128)(2,1)}, u32[]{:S(2)}, u32[]{:S(2)}) collective-permute-start(bf16[2,100,192]{2,0,1:T(2,128)(2,1)} %bitcast.174), channel_id=1, source_target_pairs={{0,4},{4,8},{8,12},{12,16},{16,20},{20,24},{24,28},{1,5},{5,9},{9,... | collective-permute-start | bytes 230408 | tf_op jit(solution)/shard_map/ppermute | solution.py:19
  303.9 5.2 collective-permute-start.8
  351.6 4.1 collective-permute-start.10
  353.2 4.1 collective-permute-start.9
  399.1 16.4 %collective-permute-start.4 = (bf16[2,100,192]{1,2,0:T(8,128)(2,1)S(1)}, bf16[2,100,192]{1,2,0:T(8,128)(2,1)}, u32[]{:S(2)}, u32[]{:S(2)}) collective-permute-start(bf16[2,100,192]{1,2,0:T(8,128)(2,1)S(1)} %fusion.106), channel_id=1, source_target_pairs={{4,0},{8,4},{12,8},{16,12},{20,16},{24,20},{28,24},{5,1},{9,5},{13... | collective-permute-start | bytes 230408 | tf_op jit(solution)/shard_map/ppermute | solution.py:19
  400.8 32.2 %collective-permute-start.5 = (bf16[2,100,192]{1,2,0:T(8,128)(2,1)S(1)}, bf16[2,100,192]{1,2,0:T(8,128)(2,1)S(1)}, u32[]{:S(2)}, u32[]{:S(2)}) collective-permute-start(bf16[2,100,192]{1,2,0:T(8,128)(2,1)S(1)} %fusion.105), channel_id=1, source_target_pairs={{4,0},{8,4},{12,8},{16,12},{20,16},{24,20},{28,24},{5,1},{9,5},{13... | collective-permute-start | bytes 230408 | tf_op jit(solution)/shard_map/ppermute | solution.py:19
  487.9 68.7 %reduce-scatter.28.cloned.1.call-start = ((), (), s32[]{:S(2)}) async-start(), calls=%async_computation.9 | async-start | bytes 768000
  514.5 45.1 %copy-start.49 = (f32[200,384]{1,0:T(8,128)}, f32[200,384]{1,0:T(8,128)S(1)}, u32[]{:S(2)}) copy-start(f32[200,384]{1,0:T(8,128)S(1)} %get-tuple-element.878) | copy-start | bytes 921604
  514.5 45.1 %copy-start.209 = (f32[200]{0:T(256)}, f32[200]{0:T(256)S(1)}, u32[]{:S(2)}) copy-start(f32[200]{0:T(256)S(1)} %negate_multiply_fusion.2) | copy-start | bytes 2404
  535.5 161.7 %reduce-scatter.30.cloned.1.call-start = ((), (), s32[]{:S(2)}) async-start(), calls=%async_computation.10 | async-start | bytes 768000
  539.6 37.7 %copy-start.174 = (bf16[96,384]{1,0:T(8,128)(2,1)S(1)}, bf16[96,384]{1,0:T(8,128)(2,1)}, u32[]{:S(2)}) copy-start(bf16[96,384]{1,0:T(8,128)(2,1)} %param.40) | copy-start | bytes 221188
  598.4 6.6 collective-permute-start.6
  599.8 12.7 %collective-permute-start.7 = (bf16[2,25,96]{2,1,0:T(8,128)(2,1)S(1)}, bf16[2,25,96]{2,1,0:T(8,128)(2,1)S(1)}, u32[]{:S(2)}, u32[]{:S(2)}) collective-permute-start(bf16[2,25,96]{2,1,0:T(8,128)(2,1)S(1)} %fusion.123), channel_id=1, source_target_pairs={{4,0},{8,4},{12,8},{16,12},{20,16},{24,20},{28,24},{5,1},{9,5},{13... | collective-permute-start | bytes 28808 | tf_op jit(solution)/shard_map/ppermute | solution.py:19
  630.1 158.5 %all-reduce.377.cloned.1.call-start = ((), (), s32[]{:S(2)}) async-start(), calls=%async_computation.5 | async-start | bytes 2359296 | tf_op jit(solution)/shard_map/psum | solution.py:512
  651.7 270.0 %all-reduce.379.cloned.1.call-start = ((), (), s32[]{:S(2)}) async-start(), calls=%async_computation.11 | async-start | bytes 233472 | tf_op jit(solution)/shard_map/psum | solution.py:512
  700.1 352.8 %all-reduce.381.cloned.1.call-start = ((), (), s32[]{:S(2)}) async-start(), calls=%async_computation.12 | async-start | bytes 15925248 | tf_op jit(solution)/shard_map/psum | solution.py:495
  921.6 138.8 %copy-start.404 = (f32[384]{0:T(512)S(1)}, f32[384]{0:T(512)}, u32[]{:S(2)}) copy-start(f32[384]{0:T(512)} %get-tuple-element.1685) | copy-start | bytes 4612
  (423 other events, 3028.8 us)
Sparse Core Ops, SparseCore 0:
  69.2 23.8 reduce-scatter.21
  116.1 22.2 reduce-scatter.23
  488.0 24.1 reduce-scatter.25
  535.6 20.9 reduce-scatter.27
  630.2 22.9 reduce-scatter.29
  659.0 129.5 all-reduce.376
  797.9 123.7 all-reduce.378
  928.2 124.7 all-reduce.380
